TPU v7x, 256 devices: a whole 4x4x8 slice. The times are simulated.
256 devices in a mesh: kv: 8 (over x, core), seq: 8 (over z), vocab: 4 (over y).
Axes of the slice: x: 4, y: 4, z: 8, core: 2. Of those that a mesh axis runs over, the one named last changes fastest.
Arguments:
- hidden_state: bfloat16 [48, 4, 3584], P('kv', 'vocab', 'seq'), may hold values from -6 to 6
- input_projection: bfloat16 [3584, 8, 1024], P('seq', 'kv'), may hold values from -0.09375 to 0.09375
- output_projection: bfloat16 [8, 512, 3584], P('kv', None, 'seq'), may hold values from -0.09375 to 0.09375
- norm_pre_attention: float32 [3584], P('seq'), may hold values from 0.1 to 1.9
- norm_post_attention: float32 [3584], P('seq'), may hold values from 0.1 to 1.9
- norm_pre_feedforward: float32 [3584], P('seq'), may hold values from 0.1 to 1.9
- norm_post_feedforward: float32 [3584], P('seq'), may hold values from 0.1 to 1.9
- norm_final: float32 [3584], P('seq'), may hold values from 0.1 to 1.9
- cache_keys: bfloat16 [4, 16384, 8, 256], P('vocab', 'seq', 'kv')
- cache_values: bfloat16 [4, 16384, 8, 256], P('vocab', 'seq', 'kv')
- cache_length: int32 [4], P('vocab'), may hold values from 1 to 16379, as said below
- ancestors: int32 [4, 48, 48], P('vocab'), may hold values from 0 to 1, as said below
- accepted_path: int32 [4, 5], P('vocab'), may hold values from 0 to 47, as said below
- gate_up_weight: bfloat16 [3584, 2, 14336], P('seq', None, ('kv', 'vocab')), may hold values from -0.09375 to 0.09375
- down_weight: bfloat16 [14336, 3584], P(('kv', 'vocab'), 'seq'), may hold values from -0.046875 to 0.046875
- draft_weight: bfloat16 [4, 3584, 3584], P(None, 'seq', ('kv', 'vocab')), may hold values from -0.09375 to 0.09375
- draft_bias: float32 [4, 3584], P(None, ('kv', 'vocab')), may hold values from -3 to 3
- vocab_weight: bfloat16 [131072, 3584], P(('kv', 'seq', 'vocab'))
- candidate_tokens: int32 [5, 48, 4, 8], replicated, may hold values from 0 to 131071
Outputs:
- keys_updated: bfloat16 [4, 16384, 8, 256], P('vocab', 'seq', 'kv')
- values_updated: bfloat16 [4, 16384, 8, 256], P('vocab', 'seq', 'kv')
- log_normalizer: float32 [5, 48, 4], replicated
- candidate_logits: float32 [5, 48, 4, 8], replicated
Inputs may be any that keep to these rules, and one draw needn't show every extreme that they name: The first cache_length[k] slots of tenant k's cache are filled; in every draw some tenant holds exactly 16379. ancestors[k, t, u] is 1 exactly when u is t or an ancestor of t in tenant k's tree; node 0 is the root and every parent has a lower index than its child. accepted_path[k] lists 5 nodes of tenant k's tree from the root down, each the parent of the next; the last of them is node 47.
All inputs are finite; a program needn't handle non-finite values.
Results may differ from a plain program's by a relative error of at most 0.02.
Values may be sent and summed in bfloat16 or wider, within the bound.
A program may use at most 64 MiB of HBM per device.

v0:
```python
import jax
import jax.numpy as jnp
from jax import lax
from jax.sharding import PartitionSpec as P

MODEL_WIDTH = 3584
HEAD_SIZE = 256
CAND = 8
EPSILON = 1e-06
SCORE_CAP = 50.0
LOGIT_CAP = 30.0


def apply_rotary(vectors, token_positions):
    half_dim = vectors.shape[-1] // 2
    frequency = 10000.0 ** (-2.0 * jnp.arange(half_dim, dtype=jnp.float32) / vectors.shape[-1])
    angles = token_positions.astype(jnp.float32)[..., None] * frequency
    cosine = jnp.cos(angles)
    sine_part = jnp.sin(angles)
    first_half = vectors[..., :half_dim]
    second_half = vectors[..., half_dim:]
    return jnp.concatenate(
        [
            first_half * cosine - second_half * sine_part,
            second_half * cosine + first_half * sine_part,
        ],
        axis=-1,
    )


def capped_weight(scores):
    return jnp.exp(SCORE_CAP * jnp.tanh(scores * 0.0625 / SCORE_CAP))


def row_inverse(values):
    totals = lax.psum(jnp.sum(values * values, axis=-1), "seq")
    return lax.rsqrt(totals / MODEL_WIDTH + EPSILON)[:, None]


def gated_units(gate_up, squares):
    inverse = lax.rsqrt(squares / MODEL_WIDTH + EPSILON)[:, None]
    return (
        jax.nn.gelu(gate_up[:, 0] * inverse, approximate=True) * (gate_up[:, 1] * inverse)
    ).astype(jnp.bfloat16)


def local(
    hidden_state,
    input_projection,
    output_projection,
    norm_pre_attention,
    norm_post_attention,
    norm_pre_feedforward,
    norm_post_feedforward,
    norm_final,
    cache_keys,
    cache_values,
    cache_length,
    ancestors,
    accepted_path,
    gate_up_weight,
    down_weight,
    draft_weight,
    draft_bias,
    vocab_weight,
    candidate_tokens,
):
    tok_block = hidden_state.shape[0]
    kv_count = lax.axis_size("kv")
    tenants = lax.axis_size("vocab")
    tree_size = tok_block * kv_count
    own_state = hidden_state[:, 0, :]
    tenant_state = lax.all_gather(own_state, "kv", axis=0, tiled=True)
    tenant_float = tenant_state.astype(jnp.float32)
    scaled_input = (tenant_float * norm_pre_attention).astype(jnp.bfloat16)
    projected_rows = jnp.einsum(
        "td,dhc->thc", scaled_input, input_projection, preferred_element_type=jnp.float32
    )
    projected_rows, squares = lax.psum(
        (projected_rows, jnp.sum(tenant_float * tenant_float, axis=-1)), "seq"
    )
    projected_rows = projected_rows * lax.rsqrt(squares / MODEL_WIDTH + EPSILON)[:, None, None]
    head_count = projected_rows.shape[1]
    depths = jnp.sum(ancestors[0], axis=-1) - 1
    length = cache_length[0]
    token_positions = length + depths
    query_rows = apply_rotary(
        projected_rows[:, :, : 2 * HEAD_SIZE].reshape(tree_size, head_count, 2, HEAD_SIZE),
        token_positions[:, None, None],
    ).astype(jnp.bfloat16)
    new_keys = apply_rotary(
        projected_rows[:, :, 2 * HEAD_SIZE : 3 * HEAD_SIZE], token_positions[:, None]
    ).astype(jnp.bfloat16)
    new_values = projected_rows[:, :, 3 * HEAD_SIZE :].astype(jnp.bfloat16)
    block_size = cache_keys.shape[1]
    block_start = lax.axis_index("seq") * block_size
    cache_cells = block_start + jnp.arange(block_size, dtype=jnp.int32)
    scores = jnp.einsum(
        "thgc,shc->thgs", query_rows, cache_keys[0], preferred_element_type=jnp.float32
    )
    weights = jnp.where((cache_cells < length)[None, None, None, :], capped_weight(scores), 0.0)
    numerator = jnp.einsum(
        "thgs,shc->thgc",
        weights.astype(jnp.bfloat16),
        cache_values[0],
        preferred_element_type=jnp.float32,
    )
    numerator, denominator = lax.psum((numerator, jnp.sum(weights, axis=-1)), "seq")
    tree_scores = jnp.einsum(
        "thgc,uhc->thgu", query_rows, new_keys, preferred_element_type=jnp.float32
    )
    tree_weights = jnp.where(ancestors[0][:, None, None, :] > 0, capped_weight(tree_scores), 0.0)
    numerator = numerator + jnp.einsum(
        "thgu,uhc->thgc",
        tree_weights.astype(jnp.bfloat16),
        new_values,
        preferred_element_type=jnp.float32,
    )
    denominator = denominator + jnp.sum(tree_weights, axis=-1)
    attended = (
        (numerator / denominator[..., None])
        .astype(jnp.bfloat16)
        .reshape(tree_size, head_count * 2 * HEAD_SIZE)
    )
    out_matrix = output_projection.reshape(head_count * 2 * HEAD_SIZE, output_projection.shape[2])
    attention_out = lax.psum_scatter(
        jnp.dot(attended, out_matrix, preferred_element_type=jnp.float32),
        "kv",
        scatter_dimension=0,
        tiled=True,
    )
    first_sum = (
        own_state.astype(jnp.float32)
        + attention_out * row_inverse(attention_out) * norm_post_attention
    ).astype(jnp.bfloat16)
    all_state = lax.all_gather(first_sum, ("kv", "vocab"), axis=0, tiled=True)
    all_float = all_state.astype(jnp.float32)
    scaled_ffn = (all_float * norm_pre_feedforward).astype(jnp.bfloat16)
    gate_up = jnp.einsum(
        "td,dcf->tcf", scaled_ffn, gate_up_weight, preferred_element_type=jnp.float32
    )
    ffn_squares = jnp.sum(all_float * all_float, axis=-1)
    gate_up, ffn_squares = lax.psum((gate_up, ffn_squares), "seq")
    activated = gated_units(gate_up, ffn_squares)
    ffn_out = lax.psum_scatter(
        jnp.dot(activated, down_weight, preferred_element_type=jnp.float32),
        ("kv", "vocab"),
        scatter_dimension=0,
        tiled=True,
    )
    first_float = first_sum.astype(jnp.float32)
    second_sum = (first_float + ffn_out * row_inverse(ffn_out) * norm_post_feedforward).astype(
        jnp.bfloat16
    )
    second_float = second_sum.astype(jnp.float32)
    normed = (second_float * row_inverse(second_float) * norm_final).astype(jnp.bfloat16)
    gathered = lax.all_gather(normed, ("kv", "vocab"), axis=0, tiled=True)
    lifted = jnp.einsum("td,ndc->tnc", gathered, draft_weight, preferred_element_type=jnp.float32)
    lifted = lax.psum(lifted.astype(jnp.bfloat16), "seq").astype(jnp.float32)
    branch = jax.nn.silu(lifted + draft_bias).astype(jnp.bfloat16)
    row_count = gathered.shape[0]
    vocab_rows = vocab_weight.shape[0]
    draft_count = branch.shape[1]
    columns = vocab_weight
    base_logits = lax.dot_general(
        lax.all_gather(gathered, "seq", axis=1, tiled=True),
        columns,
        (((1,), (1,)), ((), ())),
        preferred_element_type=jnp.float32,
    )
    columns = vocab_weight
    draft_extra = jnp.einsum(
        "tnc,vc->tnv",
        lax.all_gather(branch, ("kv", "vocab"), axis=2, tiled=True),
        columns,
        preferred_element_type=jnp.float32,
    )
    raw_logits = jnp.concatenate(
        [base_logits[:, None, :], base_logits[:, None, :] + draft_extra], axis=1
    )
    logits = LOGIT_CAP * jnp.tanh(raw_logits / LOGIT_CAP)
    totals = jnp.sum(jnp.exp(logits), axis=-1)
    head_total = draft_count + 1
    candidates = candidate_tokens.reshape(head_total, kv_count, tok_block, tenants, CAND)
    candidates = jnp.transpose(candidates, (0, 1, 3, 2, 4)).reshape(head_total, row_count, CAND)
    candidates = jnp.transpose(candidates, (1, 0, 2))
    vocab_start = lax.axis_index(("kv", "seq", "vocab")) * vocab_rows
    local_tokens = candidates - vocab_start
    entry_index = jnp.arange(vocab_rows, dtype=jnp.int32)
    picked = jnp.stack(
        [
            jnp.sum(
                jnp.where(entry_index == local_tokens[:, :, column : column + 1], logits, 0.0),
                axis=-1,
            )
            for column in range(CAND)
        ],
        axis=-1,
    )
    totals, picked = lax.psum((totals, picked), ("kv", "seq", "vocab"))
    log_totals = jnp.transpose(jnp.log(totals)).reshape(head_total, kv_count, tenants, tok_block)
    log_normalizer = jnp.transpose(log_totals, (0, 1, 3, 2)).reshape(head_total, tree_size, tenants)
    picked = jnp.transpose(picked, (1, 0, 2)).reshape(
        head_total, kv_count, tenants, tok_block, CAND
    )
    candidate_logits = jnp.transpose(picked, (0, 1, 3, 2, 4)).reshape(
        head_total, tree_size, tenants, CAND
    )
    accept_count = accepted_path.shape[1]
    slot_rows = length + jnp.arange(accept_count, dtype=jnp.int32)
    tree_nodes = jnp.arange(tree_size, dtype=jnp.int32)
    matches = (cache_cells[:, None, None] == slot_rows[None, :, None]) & (
        accepted_path[0][None, :, None] == tree_nodes[None, None, :]
    )
    selector = jnp.sum(matches.astype(jnp.float32), axis=1)
    written = jnp.sum(selector, axis=-1) > 0.0
    selector = selector.astype(jnp.bfloat16)

    def write_path(old_block, fresh_rows):
        moved_rows = jnp.dot(
            selector, fresh_rows.reshape(tree_size, -1), preferred_element_type=jnp.float32
        ).astype(jnp.bfloat16)
        return jnp.where(
            written[:, None], moved_rows, old_block[0].reshape(block_size, -1)
        ).reshape(old_block.shape)

    keys_updated = write_path(cache_keys, new_keys)
    values_updated = write_path(cache_values, new_values)
    return (keys_updated, values_updated, log_normalizer, candidate_logits)


def solution(mesh):
    placed = (
        P("kv", "vocab", "seq"),
        P("seq", "kv", None),
        P("kv", None, "seq"),
        P("seq"),
        P("seq"),
        P("seq"),
        P("seq"),
        P("seq"),
        P("vocab", "seq", "kv", None),
        P("vocab", "seq", "kv", None),
        P("vocab"),
        P("vocab", None, None),
        P("vocab", None),
        P("seq", None, ("kv", "vocab")),
        P(("kv", "vocab"), "seq"),
        P(None, "seq", ("kv", "vocab")),
        P(None, ("kv", "vocab")),
        P(("kv", "seq", "vocab"), None),
        P(),
    )
    return jax.shard_map(
        local,
        mesh=mesh,
        in_specs=placed,
        out_specs=(P("vocab", "seq", "kv", None), P("vocab", "seq", "kv", None), P(), P()),
        check_vma=False,
    )
```

profile of v0, /device:TPU:1, one launch (start us, length us, event | category | flops | bytes accessed | tf_op | source)
XLA Modules:
  0.0 775.7 jit_solution(17245792410160348582)
XLA Ops:
  7.2 0.8 copy.52
  8.1 15.8 %all-gather = bf16[48,1,448]{2,1,0:T(2,128)(2,1)S(1)} all-gather(bf16[6,1,448]{2,1,0:T(2,128)(2,1)S(1)} %copy.52), channel_id=2, replica_groups=mesh['kv'=8,'seq'=8,'vocab'=4] {'kv'}, dimensions={0}, use_global_device_ids=true | all-gather | bytes 48384 | tf_op jit(solution)/shard_map/all_gather | solution.py:73
  24.0 2.2 convolution_bitcast_fusion
  26.3 15.0 %psum.85 = f32[48]{0:T(128)S(1)} all-reduce(f32[48]{0:T(128)S(1)} %fusion.56), channel_id=1, replica_groups=mesh['kv'=8,'seq'=8,'vocab'=4] {'seq'}, use_global_device_ids=true, to_apply=%region_4.5 | all-reduce | flops 48 | bytes 384 | tf_op jit(solution)/shard_map/psum | solution.py:79
  42.0 0.7 compare_bitcast_fusion
  42.7 0.8 reduce_sum.178
  43.9 50.6 %all-reduce.10.cloned.1.call-done = f32[48,1,1024]{2,0,1:T(8,128)} async-done(((f32[48,1,1024]{2,0,1:T(8,128)}), f32[48,1,1024]{2,0,1:T(8,128)}) %all-reduce.10.cloned.1.call-update) | async-done | bytes 196624 | tf_op jit(solution)/shard_map/psum | solution.py:79
  94.5 1.0 broadcast_multiply_fusion
  95.8 1.2 fusion.93
  97.1 12.7 %psum.87 = f32[48,1,2]{0,2,1:T(2,128)S(1)} all-reduce(f32[48,1,2]{0,2,1:T(2,128)S(1)} %bitcast.224), channel_id=1, replica_groups=mesh['kv'=8,'seq'=8,'vocab'=4] {'seq'}, use_global_device_ids=true, to_apply=%region_8.9 | all-reduce | flops 96 | bytes 768 | tf_op jit(solution)/shard_map/psum | solution.py:108
  109.8 2.0 convolution_bitcast_fusion.1
  112.0 73.8 %all-reduce.12.cloned.1.call-done = f32[48,1,2,256]{3,0,2,1:T(8,128)} async-done(((f32[48,1,2,256]{3,0,2,1:T(8,128)}), f32[48,1,2,256]{3,0,2,1:T(8,128)}) %all-reduce.12.cloned.1.call-update) | async-done | bytes 98320 | tf_op jit(solution)/shard_map/psum | solution.py:108
  185.8 1.1 fusion.24
  187.0 0.2 fusion.35
  187.3 18.1 %fusion = f32[8,448]{1,0:T(8,128)S(1)} fusion(f32[48,448]{1,0:T(8,128)S(1)} %fusion.35), kind=kCustom, calls=%all-reduce-scatter | all-reduce-scatter fusion | flops 28673 | bytes 101376
  205.3 3.4 collective-permute-start
  208.8 1.6 collective-permute-start.1
  210.4 0.6 dynamic-slice.6
  212.0 11.6 %psum.88 = f32[6]{0:T(128)S(1)} all-reduce(f32[6]{0:T(128)S(1)} %multiply_reduce_fusion.2), channel_id=1, replica_groups=mesh['kv'=8,'seq'=8,'vocab'=4] {'seq'}, use_global_device_ids=true, to_apply=%region_12.13 | all-reduce | flops 6 | bytes 48 | tf_op jit(solution)/shard_map/psum | solution.py:36
  223.7 45.5 %all-gather.1 = bf16[32,6,448]{2,1,0:T(8,128)(2,1)S(1)} all-gather(bf16[1,6,448]{2,1,0:T(8,128)(2,1)S(1)} %bitcast.223), channel_id=1, replica_groups=mesh['kv'=8,'seq'=8,'vocab'=4] {'kv','vocab'}, dimensions={0}, use_global_device_ids=true | all-gather | bytes 177408 | tf_op jit(solution)/shard_map/all_gather | solution.py:136
  269.4 1.3 fusion.33
  270.8 11.5 %psum.90 = f32[192]{0:T(256)S(1)} all-reduce(f32[192]{0:T(256)S(1)} %multiply_reduce_fusion), channel_id=1, replica_groups=mesh['kv'=8,'seq'=8,'vocab'=4] {'seq'}, use_global_device_ids=true, to_apply=%region_15.16 | all-reduce | flops 192 | bytes 1536 | tf_op jit(solution)/shard_map/psum | solution.py:143
  282.3 57.1 %all-reduce.14.cloned.1.call-done = f32[192,2,448]{2,0,1:T(8,128)} async-done(((f32[192,2,448]{2,0,1:T(8,128)}), f32[192,2,448]{2,0,1:T(8,128)}) %all-reduce.14.cloned.1.call-update) | async-done | bytes 688144 | tf_op jit(solution)/shard_map/psum | solution.py:143
  339.4 1.6 fusion.53
  341.1 68.1 %fusion.1 = f32[8,448]{1,0:T(8,128)S(1)} fusion(f32[192,448]{1,0:T(8,128)S(1)} %fusion.53), kind=kCustom, calls=%all-reduce-scatter.1 | all-reduce-scatter fusion | flops 114689 | bytes 359424
  409.1 1.9 collective-permute-start.2
  411.1 1.9 collective-permute-start.3
  413.0 1.4 collective-permute-start.9
  414.4 1.9 collective-permute-start.4
  416.4 1.9 collective-permute-start.5
  418.3 5.9 collective-permute-start.6
  424.2 6.8 collective-permute-start.7
  431.0 3.9 collective-permute-start.8
  435.0 0.6 dynamic-slice.10
  436.3 0.8 concatenate.35
  437.2 12.6 %psum.91 = f32[6]{0:T(128)S(1)} all-reduce(f32[6]{0:T(128)S(1)} %multiply_reduce_fusion.1), channel_id=1, replica_groups=mesh['kv'=8,'seq'=8,'vocab'=4] {'seq'}, use_global_device_ids=true, to_apply=%region_18.19 | all-reduce | flops 6 | bytes 48 | tf_op jit(solution)/shard_map/psum | solution.py:36
  450.0 10.7 %psum.92 = f32[6]{0:T(128)S(1)} all-reduce(f32[6]{0:T(128)S(1)} %get-tuple-element.17), channel_id=1, replica_groups=mesh['kv'=8,'seq'=8,'vocab'=4] {'seq'}, use_global_device_ids=true, to_apply=%region_20.21 | all-reduce | flops 6 | bytes 48 | tf_op jit(solution)/shard_map/psum | solution.py:36
  460.8 48.2 %all-gather.2 = bf16[32,6,448]{2,1,0:T(8,128)(2,1)S(1)} all-gather(bf16[1,6,448]{2,1,0:T(8,128)(2,1)S(1)} %fusion.82), channel_id=1, replica_groups=mesh['kv'=8,'seq'=8,'vocab'=4] {'kv','vocab'}, dimensions={0}, use_global_device_ids=true | all-gather | bytes 177408 | tf_op jit(solution)/shard_map/all_gather | solution.py:157
  509.1 0.9 convolution_convert_fusion.2
  510.2 0.8 reshape.410
  511.0 0.2 all-gather.7.cloned.1.call-start
  511.2 64.1 %all-reduce.16.cloned.1.call-done = bf16[192,4,112]{2,0,1:T(8,128)(2,1)} async-done(((bf16[192,4,112]{2,0,1:T(8,128)(2,1)}), bf16[192,4,112]{2,0,1:T(8,128)(2,1)}) %all-reduce.16.cloned.1.call-update) | async-done | bytes 172048 | tf_op jit(solution)/shard_map/psum | solution.py:159
  575.3 1.0 multiply_convert_fusion
  576.3 0.9 copy.60
  577.5 0.4 copy.63
  577.9 0.6 sub.35
  578.7 0.3 convert_reduce_fusion
  579.1 0.6 copy_bitcast_fusion
  579.7 0.6 copy_bitcast_fusion.2
  580.3 0.6 copy_bitcast_fusion.4
  580.9 0.6 copy_bitcast_fusion.6
  581.5 2.5 fusion.6
  584.1 1.5 fusion.8
  585.5 30.5 %all-gather.9.cloned.1.call-done = bf16[8,448,192]{1,2,0:T(8,128)(2,1)} async-done(((bf16[1,448,192]{1,2,0:T(8,128)(2,1)}), bf16[8,448,192]{1,2,0:T(8,128)(2,1)}) %all-gather.9.cloned.1.call-update) | async-done | bytes 1376272 | tf_op jit(solution)/shard_map/all_gather | solution.py:166
  616.1 2.3 copy.59
  618.4 2.7 reshape.412
  621.1 3.8 fusion.95
  625.0 52.4 %all-gather.7.cloned.1.call-done = bf16[192,4,3584]{0,1,2:T(4,128)(2,1)} async-done(((bf16[192,4,112]{0,1,2:T(4,128)(2,1)}), bf16[192,4,3584]{0,1,2:T(4,128)(2,1)}) %all-gather.7.cloned.1.call-update) | async-done | bytes 5505040 | tf_op jit(solution)/shard_map/all_gather | solution.py:174
  677.3 8.2 %fusion.17 = f32[192,4,512]{2,0,1:T(8,128)S(1)} fusion(bf16[512,3584]{1,0:T(8,128)(2,1)} %param.36, bf16[192,4,3584]{0,1,2:T(4,128)(2,1)} %all-gather.7.cloned.1.call-done, f32[192,512]{1,0:T(8,128)S(1)} %fusion.95), kind=kOutput, calls=%fused_computation.38 | convolution fusion | flops 2818965504 | bytes 11141120 | tf_op jit(solution)/shard_map/tnc,vc->tnv/dot_general | solution.py:172
  685.6 4.4 select_reduce_fusion
  690.2 0.8 reshape.400
  691.2 0.2 reshape.401
  691.4 76.6 %all-reduce.4 = (f32[192,5]{0,1:T(8,128)S(1)}, f32[5,48,4,8]{1,3,2,0:T(8,128)}) all-reduce(f32[192,5]{0,1:T(8,128)S(1)} %get-tuple-element.19, f32[5,48,4,8]{1,3,2,0:T(8,128)S(1)} %reshape.401), channel_id=1, replica_groups=mesh['kv'=8,'seq'=8,'vocab'=4] {'kv','seq','vocab'}, use_global_device_ids=true, to_apply=%region_23.24 | all-reduce | flops 8640 | bytes 69120 | tf_op jit(solution)/shard_map/psum | solution.py:200
  768.1 0.7 reshape.399
  (118 shorter events, 3.5 us)
Async XLA Ops:
  7.2 262.2 %copy-start = (bf16[448,2,448]{2,1,0:T(2,128)(2,1)S(1)}, bf16[448,2,448]{2,1,0:T(2,128)(2,1)}, u32[]{:S(2)}) copy-start(bf16[448,2,448]{2,1,0:T(2,128)(2,1)} %param.32) | copy-start | bytes 2408452
  7.2 88.7 %copy-start.2 = (bf16[1,2048,1,256]{3,1,2,0:T(8,128)(2,1)S(1)}, bf16[1,2048,1,256]{3,1,2,0:T(8,128)(2,1)}, u32[]{:S(2)}) copy-start(bf16[1,2048,1,256]{3,1,2,0:T(8,128)(2,1)} %param.27) | copy-start | bytes 3145732
  7.2 87.3 %all-reduce.10.cloned.1.call-start = ((), (), s32[]{:S(2)}) async-start(), calls=%async_computation | async-start | bytes 393216 | tf_op jit(solution)/shard_map/psum | solution.py:79
  26.1 83.6 %copy-start.1 = (bf16[1,2048,1,256]{3,1,2,0:T(8,128)(2,1)S(1)}, bf16[1,2048,1,256]{3,1,2,0:T(8,128)(2,1)}, u32[]{:S(2)}) copy-start(bf16[1,2048,1,256]{3,1,2,0:T(8,128)(2,1)} %param.28) | copy-start | bytes 3145732
  26.2 159.7 %all-reduce.12.cloned.1.call-start = ((), (), s32[]{:S(2)}) async-start(), calls=%async_computation.1 | async-start | bytes 196608 | tf_op jit(solution)/shard_map/psum | solution.py:108
  97.1 89.9 %copy-start.3 = (bf16[1,512,448]{1,2,0:T(8,128)(2,1)S(1)}, bf16[1,512,448]{1,2,0:T(8,128)(2,1)}, u32[]{:S(2)}) copy-start(bf16[1,512,448]{1,2,0:T(8,128)(2,1)} %param.21) | copy-start | bytes 1376260
  97.1 113.3 %copy-start.20 = (u32[256]{0:T(256)S(1)}, u32[256]{0:T(256)}, u32[]{:S(2)}) copy-start(u32[256]{0:T(256)} %constant.87) | copy-start | bytes 3076
  97.1 126.5 %copy-start.13 = (bf16[6,1,448]{2,0,1:T(8,128)(2,1)S(1)}, bf16[6,1,448]{2,0,1:T(8,128)(2,1)}, u32[]{:S(2)}) copy-start(bf16[6,1,448]{2,0,1:T(8,128)(2,1)} %param.19) | copy-start | bytes 16132
  97.1 126.5 %copy-start.16 = (f32[448]{0:T(512)S(1)}, f32[448]{0:T(512)}, u32[]{:S(2)}) copy-start(f32[448]{0:T(512)} %param.23) | copy-start | bytes 5380
  109.8 159.6 %copy-start.14 = (f32[448]{0:T(512)S(1)}, f32[448]{0:T(512)}, u32[]{:S(2)}) copy-start(f32[448]{0:T(512)} %param.24) | copy-start | bytes 5380
  111.8 227.7 %all-reduce.14.cloned.1.call-start = ((), (), s32[]{:S(2)}) async-start(), calls=%async_computation.2 | async-start | bytes 1572864 | tf_op jit(solution)/shard_map/psum | solution.py:143
  205.3 6.3 collective-permute-start
  208.8 2.8 collective-permute-start.1
  270.6 164.4 %copy-start.19 = (u32[256]{0:T(256)S(1)}, u32[256]{0:T(256)}, u32[]{:S(2)}) copy-start(u32[256]{0:T(256)} %constant.91) | copy-start | bytes 3076
  270.6 179.2 %copy-start.17 = (f32[448]{0:T(512)S(1)}, f32[448]{0:T(512)}, u32[]{:S(2)}) copy-start(f32[448]{0:T(512)} %param.25) | copy-start | bytes 5380
  270.6 190.1 %copy-start.18 = (f32[448]{0:T(512)S(1)}, f32[448]{0:T(512)}, u32[]{:S(2)}) copy-start(f32[448]{0:T(512)} %param.26) | copy-start | bytes 5380
  270.6 238.5 %copy-start.4 = (bf16[4,448,112]{2,1,0:T(8,128)(2,1)S(1)}, bf16[4,448,112]{2,1,0:T(8,128)(2,1)}, u32[]{:S(2)}) copy-start(bf16[4,448,112]{2,1,0:T(8,128)(2,1)} %param.34) | copy-start | bytes 1204228
  270.7 304.6 %all-reduce.16.cloned.1.call-start = ((), (), s32[]{:S(2)}) async-start(), calls=%async_computation.3 | async-start | bytes 393216 | tf_op jit(solution)/shard_map/psum | solution.py:159
  341.1 234.2 %copy-start.15 = (f32[4,112]{1,0:T(4,128)S(1)}, f32[4,112]{1,0:T(4,128)}, u32[]{:S(2)}) copy-start(f32[4,112]{1,0:T(4,128)} %param.35) | copy-start | bytes 5380
  409.1 15.1 %collective-permute-start.2 = (f32[8,448]{1,0:T(8,128)S(1)}, f32[8,448]{1,0:T(8,128)S(1)}, u32[]{:S(2)}, u32[]{:S(2)}) collective-permute-start(f32[8,448]{1,0:T(8,128)S(1)} %fusion.1), channel_id=1, source_target_pairs={{0,1},{1,2},{2,3},{3,32},{32,33},{33,34},{34,35},{35,64},{64,65},{... | collective-permute-start | bytes 43016
  411.1 20.0 %collective-permute-start.3 = (f32[8,448]{1,0:T(8,128)S(1)}, f32[8,448]{1,0:T(8,128)S(1)}, u32[]{:S(2)}, u32[]{:S(2)}) collective-permute-start(f32[8,448]{1,0:T(8,128)S(1)} %fusion.1), channel_id=1, source_target_pairs={{0,2},{1,3},{2,32},{3,33},{32,34},{33,35},{34,64},{35,65},{64,66},... | collective-permute-start | bytes 43016
  413.0 164.3 %copy-start.5 = (s32[5,48,4,8]{1,3,2,0:T(8,128)S(1)}, s32[5,48,4,8]{1,3,2,0:T(8,128)}, u32[]{:S(2)}) copy-start(s32[5,48,4,8]{1,3,2,0:T(8,128)} %param.37) | copy-start | bytes 92164
  413.0 5.3 collective-permute-start.9
  414.4 21.8 %collective-permute-start.4 = (f32[8,448]{1,0:T(8,128)S(1)}, f32[8,448]{1,0:T(8,128)S(1)}, u32[]{:S(2)}, u32[]{:S(2)}) collective-permute-start(f32[8,448]{1,0:T(8,128)S(1)} %fusion.1), channel_id=1, source_target_pairs={{0,3},{1,32},{2,33},{3,34},{32,35},{33,64},{34,65},{35,66},{64,67}... | collective-permute-start | bytes 43016
  416.4 19.9 %collective-permute-start.5 = (f32[8,448]{1,0:T(8,128)S(1)}, f32[8,448]{1,0:T(8,128)S(1)}, u32[]{:S(2)}, u32[]{:S(2)}) collective-permute-start(f32[8,448]{1,0:T(8,128)S(1)} %fusion.1), channel_id=1, source_target_pairs={{0,32},{1,33},{2,34},{3,35},{32,64},{33,65},{34,66},{35,67},{64,96... | collective-permute-start | bytes 43016
  418.3 17.9 %collective-permute-start.6 = (f32[8,448]{1,0:T(8,128)S(1)}, f32[8,448]{1,0:T(8,128)S(1)}, u32[]{:S(2)}, u32[]{:S(2)}) collective-permute-start(f32[8,448]{1,0:T(8,128)S(1)} %fusion.1), channel_id=1, source_target_pairs={{0,33},{1,34},{2,35},{3,64},{32,65},{33,66},{34,67},{35,96},{64,97... | collective-permute-start | bytes 43016
  424.2 12.1 %collective-permute-start.7 = (f32[8,448]{1,0:T(8,128)S(1)}, f32[8,448]{1,0:T(8,128)S(1)}, u32[]{:S(2)}, u32[]{:S(2)}) collective-permute-start(f32[8,448]{1,0:T(8,128)S(1)} %fusion.1), channel_id=1, source_target_pairs={{0,34},{1,35},{2,64},{3,65},{32,66},{33,67},{34,96},{35,97},{64,98... | collective-permute-start | bytes 43016
  431.0 5.2 collective-permute-start.8
  510.1 106.0 %all-gather.9.cloned.1.call-start = ((), (), s32[]{:S(2)}) async-start(), calls=%async_computation.5 | async-start | bytes 1769472 | tf_op jit(solution)/shard_map/all_gather | solution.py:166
  511.0 67.6 %copy-start.21 = (s32[1,5]{1,0:T(1,128)S(1)}, s32[1,5]{1,0:T(1,128)}, u32[]{:S(2)}) copy-start(s32[1,5]{1,0:T(1,128)} %param.31) | copy-start | bytes 64
  511.0 166.3 %all-gather.7.cloned.1.call-start = ((), (), s32[]{:S(2)}) async-start(), calls=%async_computation.4 | async-start | bytes 7569408 | tf_op jit(solution)/shard_map/all_gather | solution.py:174
  624.9 60.7 %copy-start.6 = (s32[192,5]{0,1:T(8,128)S(1)}, s32[192,5]{0,1:T(8,128)}, u32[]{:S(2)}) copy-start(s32[192,5]{0,1:T(8,128)} %get-tuple-element.43) | copy-start | bytes 11524
  624.9 60.7 %copy-start.7 = (s32[192,5]{0,1:T(8,128)S(1)}, s32[192,5]{0,1:T(8,128)}, u32[]{:S(2)}) copy-start(s32[192,5]{0,1:T(8,128)} %get-tuple-element.44) | copy-start | bytes 11524
  624.9 60.7 %copy-start.8 = (s32[192,5]{0,1:T(8,128)S(1)}, s32[192,5]{0,1:T(8,128)}, u32[]{:S(2)}) copy-start(s32[192,5]{0,1:T(8,128)} %get-tuple-element.45) | copy-start | bytes 11524
  624.9 60.7 %copy-start.9 = (s32[192,5]{0,1:T(8,128)S(1)}, s32[192,5]{0,1:T(8,128)}, u32[]{:S(2)}) copy-start(s32[192,5]{0,1:T(8,128)} %get-tuple-element.46) | copy-start | bytes 11524
  624.9 60.7 %copy-start.10 = (s32[192,5]{0,1:T(8,128)S(1)}, s32[192,5]{0,1:T(8,128)}, u32[]{:S(2)}) copy-start(s32[192,5]{0,1:T(8,128)} %get-tuple-element.47) | copy-start | bytes 11524
  624.9 60.7 %copy-start.11 = (s32[192,5]{0,1:T(8,128)S(1)}, s32[192,5]{0,1:T(8,128)}, u32[]{:S(2)}) copy-start(s32[192,5]{0,1:T(8,128)} %get-tuple-element.48) | copy-start | bytes 11524
  625.0 60.7 %copy-start.12 = (s32[192,5]{0,1:T(8,128)S(1)}, s32[192,5]{0,1:T(8,128)}, u32[]{:S(2)}) copy-start(s32[192,5]{0,1:T(8,128)} %get-tuple-element.49) | copy-start | bytes 11524
Sparse Core Ops, SparseCore 0:
  26.3 68.1 all-reduce.9
  111.9 73.9 all-reduce.11
  270.8 68.6 all-reduce.13
  510.2 65.0 all-reduce.15
  576.9 39.1 all-gather.8
  618.5 58.7 all-gather.6
where the time goes:
time: 777 us; the launch traced here: 776 us
  blocking collectives  346 us (45%)
  waiting for transfers between devices  329 us (42%)
  starting transfers between devices  31.2 us (4%)
  matrix products  26.7 us (3%)
  between operations  16.9 us (2%)
  local copies, waits for them, and re-layouts  16 us (2%)
  other arithmetic  9.93 us (1%)
    unnamed x2, blocking collectives  86.2 us
    psum x1, blocking collectives, local(): totals, picked = lax.psum((totals, picked), ('kv', 'seq', 'vocab'))  76.6 us
    psum x1, waiting for transfers between devices, local(): lax.psum((numerator, jnp.sum(weights, axis=-1)), 'seq')  73.8 us
    psum x1, waiting for transfers between devices, local(): lifted = lax.psum(lifted.astype(jnp.bfloat16), 'seq').astype(jnp.float32)  64.1 us
    psum x1, waiting for transfers between devices, local(): gate_up, ffn_squares = lax.psum((gate_up, ffn_squares), 'seq')  57.1 us
    all_gather x1, waiting for transfers between devices, local(): lax.all_gather(branch, ('kv', 'vocab'), axis=2, tiled=True)  52.4 us
    psum x1, waiting for transfers between devices, local(): lax.psum((projected_rows, jnp.sum(tenant_float * tenant_float, axis=-1)),...  50.6 us
    all_gather x1, blocking collectives, local(): gathered = lax.all_gather(normed, ('kv', 'vocab'), axis=0, tiled=True)  48.2 us
  transfers between devices with their start and end apart: 16, of which 6 were waited for; matrix products, arithmetic and copies ran while one was open for 3% of the time, Pallas kernels for 0%

commit v1 on v0

--- a/solution.py
+++ b/solution.py
@@ -33,7 +33,7 @@
 
 
 def row_inverse(values):
-    totals = lax.psum(jnp.sum(values * values, axis=-1), "seq")
+    totals = jnp.sum(lax.all_gather(jnp.sum(values * values, axis=-1), "seq"), axis=0)
     return lax.rsqrt(totals / MODEL_WIDTH + EPSILON)[:, None]
 
 

time: 777 us -> 779 us (level)
    psum x3 -> x0, blocking collectives: 34.9 us -> none  [row_inverse(): totals = lax.psum(jnp.sum(values * values, axis=-1), 'seq')]
    unnamed x2 -> x5, blocking collectives: 86.2 us -> 121 us
where the time goes in v1:
time: 779 us; the launch traced here: 778 us
  blocking collectives  346 us (44%)
  waiting for transfers between devices  329 us (42%)
  starting transfers between devices  31 us (4%)
  matrix products  26.7 us (3%)
  local copies, waits for them, and re-layouts  17.6 us (2%)
  between operations  17.6 us (2%)
  other arithmetic  10 us (1%)
    unnamed x5, blocking collectives  121 us
    psum x1, blocking collectives, local(): totals, picked = lax.psum((totals, picked), ('kv', 'seq', 'vocab'))  76.6 us
    psum x1, waiting for transfers between devices, local(): lax.psum((numerator, jnp.sum(weights, axis=-1)), 'seq')  73.9 us
    psum x1, waiting for transfers between devices, local(): lifted = lax.psum(lifted.astype(jnp.bfloat16), 'seq').astype(jnp.float32)  64.1 us
    psum x1, waiting for transfers between devices, local(): gate_up, ffn_squares = lax.psum((gate_up, ffn_squares), 'seq')  57 us
    all_gather x1, waiting for transfers between devices, local(): lax.all_gather(branch, ('kv', 'vocab'), axis=2, tiled=True)  52.4 us
    psum x1, waiting for transfers between devices, local(): lax.psum((projected_rows, jnp.sum(tenant_float * tenant_float, axis=-1)),...  50.6 us
    all_gather x1, blocking collectives, local(): gathered = lax.all_gather(normed, ('kv', 'vocab'), axis=0, tiled=True)  48.2 us
  transfers between devices with their start and end apart: 16, of which 6 were waited for; matrix products, arithmetic and copies ran while one was open for 3% of the time, Pallas kernels for 0%

profile of v1, /device:TPU:1, one launch (start us, length us, event | category | flops | bytes accessed | tf_op | source)
XLA Modules:
  0.0 777.7 jit_solution(16809206044186764168)
XLA Ops:
  7.2 0.8 copy.52
  8.1 15.8 %all-gather = bf16[48,1,448]{2,1,0:T(2,128)(2,1)S(1)} all-gather(bf16[6,1,448]{2,1,0:T(2,128)(2,1)S(1)} %copy.52), channel_id=2, replica_groups=mesh['kv'=8,'seq'=8,'vocab'=4] {'kv'}, dimensions={0}, use_global_device_ids=true | all-gather | bytes 48384 | tf_op jit(solution)/shard_map/all_gather | solution.py:73
  24.0 2.2 convolution_bitcast_fusion
  26.3 15.0 %psum.64 = f32[48]{0:T(128)S(1)} all-reduce(f32[48]{0:T(128)S(1)} %fusion.56), channel_id=1, replica_groups=mesh['kv'=8,'seq'=8,'vocab'=4] {'seq'}, use_global_device_ids=true, to_apply=%region_4.5 | all-reduce | flops 48 | bytes 384 | tf_op jit(solution)/shard_map/psum | solution.py:79
  42.0 0.7 compare_bitcast_fusion
  42.7 0.8 reduce_sum.205
  43.9 50.6 %all-reduce.13.cloned.1.call-done = f32[48,1,1024]{2,0,1:T(8,128)} async-done(((f32[48,1,1024]{2,0,1:T(8,128)}), f32[48,1,1024]{2,0,1:T(8,128)}) %all-reduce.13.cloned.1.call-update) | async-done | bytes 196624 | tf_op jit(solution)/shard_map/psum | solution.py:79
  94.5 1.0 broadcast_multiply_fusion
  95.8 1.2 fusion.93
  97.1 12.7 %psum.66 = f32[48,1,2]{0,2,1:T(2,128)S(1)} all-reduce(f32[48,1,2]{0,2,1:T(2,128)S(1)} %bitcast.225), channel_id=1, replica_groups=mesh['kv'=8,'seq'=8,'vocab'=4] {'seq'}, use_global_device_ids=true, to_apply=%region_8.9 | all-reduce | flops 96 | bytes 768 | tf_op jit(solution)/shard_map/psum | solution.py:108
  109.8 2.0 convolution_bitcast_fusion.1
  112.0 73.9 %all-reduce.15.cloned.1.call-done = f32[48,1,2,256]{3,0,2,1:T(8,128)} async-done(((f32[48,1,2,256]{3,0,2,1:T(8,128)}), f32[48,1,2,256]{3,0,2,1:T(8,128)}) %all-reduce.15.cloned.1.call-update) | async-done | bytes 98320 | tf_op jit(solution)/shard_map/psum | solution.py:108
  185.9 1.1 fusion.24
  187.3 18.1 %fusion = f32[8,448]{1,0:T(8,128)S(1)} fusion(f32[48,448]{1,0:T(8,128)S(1)} %fusion.35), kind=kCustom, calls=%all-reduce-scatter | all-reduce-scatter fusion | flops 28673 | bytes 101376
  205.4 3.4 collective-permute-start
  208.9 1.6 collective-permute-start.1
  210.4 0.6 dynamic-slice.9
  211.7 0.6 dynamic-slice
  213.3 0.2 dynamic-update-slice
  213.5 11.5 %all-reduce = f32[48]{0:T(128)S(1)} all-reduce(f32[48]{0:T(128)S(1)} %dynamic-update-slice), channel_id=3, replica_groups=mesh['kv'=8,'seq'=8,'vocab'=4] {'seq'}, use_global_device_ids=true, to_apply=%add | all-reduce | flops 48 | bytes 384
  225.2 45.5 %all-gather.4 = bf16[32,6,448]{2,1,0:T(8,128)(2,1)S(1)} all-gather(bf16[1,6,448]{2,1,0:T(8,128)(2,1)S(1)} %bitcast.224), channel_id=1, replica_groups=mesh['kv'=8,'seq'=8,'vocab'=4] {'kv','vocab'}, dimensions={0}, use_global_device_ids=true | all-gather | bytes 177408 | tf_op jit(solution)/shard_map/all_gather | solution.py:136
  270.9 1.3 fusion.33
  272.3 11.5 %psum.68 = f32[192]{0:T(256)S(1)} all-reduce(f32[192]{0:T(256)S(1)} %multiply_reduce_fusion), channel_id=1, replica_groups=mesh['kv'=8,'seq'=8,'vocab'=4] {'seq'}, use_global_device_ids=true, to_apply=%region_15.16 | all-reduce | flops 192 | bytes 1536 | tf_op jit(solution)/shard_map/psum | solution.py:143
  283.8 57.0 %all-reduce.17.cloned.1.call-done = f32[192,2,448]{2,0,1:T(8,128)} async-done(((f32[192,2,448]{2,0,1:T(8,128)}), f32[192,2,448]{2,0,1:T(8,128)}) %all-reduce.17.cloned.1.call-update) | async-done | bytes 688144 | tf_op jit(solution)/shard_map/psum | solution.py:143
  340.9 1.6 fusion.53
  342.5 68.1 %fusion.1 = f32[8,448]{1,0:T(8,128)S(1)} fusion(f32[192,448]{1,0:T(8,128)S(1)} %fusion.53), kind=kCustom, calls=%all-reduce-scatter.1 | all-reduce-scatter fusion | flops 114689 | bytes 359424
  410.6 1.9 collective-permute-start.2
  412.5 1.9 collective-permute-start.3
  414.5 1.3 collective-permute-start.9
  415.8 1.9 collective-permute-start.4
  417.7 1.9 collective-permute-start.5
  419.6 5.9 collective-permute-start.6
  425.5 6.8 collective-permute-start.7
  432.4 3.9 collective-permute-start.8
  436.3 0.6 dynamic-slice.13
  437.6 0.8 concatenate.35
  438.5 0.2 dynamic-update-slice.1
  438.8 12.6 %all-reduce.1 = f32[48]{0:T(128)S(1)} all-reduce(f32[48]{0:T(128)S(1)} %dynamic-update-slice.1), channel_id=4, replica_groups=mesh['kv'=8,'seq'=8,'vocab'=4] {'seq'}, use_global_device_ids=true, to_apply=%add.1 | all-reduce | flops 48 | bytes 384
  451.9 10.7 %all-reduce.2 = f32[48]{0:T(128)S(1)} all-reduce(f32[48]{0:T(128)S(1)} %dynamic-update-slice.2), channel_id=5, replica_groups=mesh['kv'=8,'seq'=8,'vocab'=4] {'seq'}, use_global_device_ids=true, to_apply=%add.2 | all-reduce | flops 48 | bytes 384
  462.8 48.2 %all-gather.5 = bf16[32,6,448]{2,1,0:T(8,128)(2,1)S(1)} all-gather(bf16[1,6,448]{2,1,0:T(8,128)(2,1)S(1)} %fusion.82), channel_id=1, replica_groups=mesh['kv'=8,'seq'=8,'vocab'=4] {'kv','vocab'}, dimensions={0}, use_global_device_ids=true | all-gather | bytes 177408 | tf_op jit(solution)/shard_map/all_gather | solution.py:157
  511.1 0.9 convolution_convert_fusion.2
  512.2 0.8 reshape.434
  513.2 64.1 %all-reduce.19.cloned.1.call-done = bf16[192,4,112]{2,0,1:T(8,128)(2,1)} async-done(((bf16[192,4,112]{2,0,1:T(8,128)(2,1)}), bf16[192,4,112]{2,0,1:T(8,128)(2,1)}) %all-reduce.19.cloned.1.call-update) | async-done | bytes 172048 | tf_op jit(solution)/shard_map/psum | solution.py:159
  577.3 1.0 multiply_convert_fusion
  578.3 0.9 copy.60
  579.5 0.4 copy.63
  579.9 0.6 sub.35
  580.7 0.3 convert_reduce_fusion
  581.1 0.6 copy_bitcast_fusion
  581.7 0.6 copy_bitcast_fusion.2
  582.3 0.6 copy_bitcast_fusion.4
  582.9 0.6 copy_bitcast_fusion.6
  583.5 2.5 fusion.6
  586.0 1.5 fusion.8
  587.5 30.6 %all-gather.12.cloned.1.call-done = bf16[8,448,192]{1,2,0:T(8,128)(2,1)} async-done(((bf16[1,448,192]{1,2,0:T(8,128)(2,1)}), bf16[8,448,192]{1,2,0:T(8,128)(2,1)}) %all-gather.12.cloned.1.call-update) | async-done | bytes 1376272 | tf_op jit(solution)/shard_map/all_gather | solution.py:166
  618.1 2.3 copy.59
  620.4 2.7 reshape.436
  623.1 3.8 fusion.95
  627.0 52.4 %all-gather.10.cloned.1.call-done = bf16[192,4,3584]{0,1,2:T(4,128)(2,1)} async-done(((bf16[192,4,112]{0,1,2:T(4,128)(2,1)}), bf16[192,4,3584]{0,1,2:T(4,128)(2,1)}) %all-gather.10.cloned.1.call-update) | async-done | bytes 5505040 | tf_op jit(solution)/shard_map/all_gather | solution.py:174
  679.3 8.2 %fusion.17 = f32[192,4,512]{2,0,1:T(8,128)S(1)} fusion(bf16[512,3584]{1,0:T(8,128)(2,1)} %param.36, bf16[192,4,3584]{0,1,2:T(4,128)(2,1)} %all-gather.10.cloned.1.call-done, f32[192,512]{1,0:T(8,128)S(1)} %fusion.95), kind=kOutput, calls=%fused_computation.38 | convolution fusion | flops 2818965504 | bytes 11141120 | tf_op jit(solution)/shard_map/tnc,vc->tnv/dot_general | solution.py:172
  687.6 4.4 select_reduce_fusion
  692.2 0.8 reshape.412
  693.4 76.6 %all-reduce.7 = (f32[192,5]{0,1:T(8,128)S(1)}, f32[5,48,4,8]{1,3,2,0:T(8,128)}) all-reduce(f32[192,5]{0,1:T(8,128)S(1)} %get-tuple-element.19, f32[5,48,4,8]{1,3,2,0:T(8,128)S(1)} %reshape.413), channel_id=1, replica_groups=mesh['kv'=8,'seq'=8,'vocab'=4] {'kv','seq','vocab'}, use_global_device_ids=true, to_apply=%region_23.24 | all-reduce | flops 8640 | bytes 69120 | tf_op jit(solution)/shard_map/psum | solution.py:200
  770.1 0.7 reshape.411
  (133 shorter events, 4.7 us)
Async XLA Ops:
  7.2 263.7 %copy-start = (bf16[448,2,448]{2,1,0:T(2,128)(2,1)S(1)}, bf16[448,2,448]{2,1,0:T(2,128)(2,1)}, u32[]{:S(2)}) copy-start(bf16[448,2,448]{2,1,0:T(2,128)(2,1)} %param.32) | copy-start | bytes 2408452
  7.2 88.7 %copy-start.2 = (bf16[1,2048,1,256]{3,1,2,0:T(8,128)(2,1)S(1)}, bf16[1,2048,1,256]{3,1,2,0:T(8,128)(2,1)}, u32[]{:S(2)}) copy-start(bf16[1,2048,1,256]{3,1,2,0:T(8,128)(2,1)} %param.27) | copy-start | bytes 3145732
  7.2 87.3 %all-reduce.13.cloned.1.call-start = ((), (), s32[]{:S(2)}) async-start(), calls=%async_computation | async-start | bytes 393216 | tf_op jit(solution)/shard_map/psum | solution.py:79
  26.1 83.6 %copy-start.1 = (bf16[1,2048,1,256]{3,1,2,0:T(8,128)(2,1)S(1)}, bf16[1,2048,1,256]{3,1,2,0:T(8,128)(2,1)}, u32[]{:S(2)}) copy-start(bf16[1,2048,1,256]{3,1,2,0:T(8,128)(2,1)} %param.28) | copy-start | bytes 3145732
  26.2 159.7 %all-reduce.15.cloned.1.call-start = ((), (), s32[]{:S(2)}) async-start(), calls=%async_computation.1 | async-start | bytes 196608 | tf_op jit(solution)/shard_map/psum | solution.py:108
  97.1 90.0 %copy-start.3 = (bf16[1,512,448]{1,2,0:T(8,128)(2,1)S(1)}, bf16[1,512,448]{1,2,0:T(8,128)(2,1)}, u32[]{:S(2)}) copy-start(bf16[1,512,448]{1,2,0:T(8,128)(2,1)} %param.21) | copy-start | bytes 1376260
  97.1 113.3 %copy-start.20 = (u32[256]{0:T(256)S(1)}, u32[256]{0:T(256)}, u32[]{:S(2)}) copy-start(u32[256]{0:T(256)} %constant.105) | copy-start | bytes 3076
  97.1 114.6 %copy-start.22 = (u32[256]{0:T(256)S(1)}, u32[256]{0:T(256)}, u32[]{:S(2)}) copy-start(u32[256]{0:T(256)} %constant.87) | copy-start | bytes 3076
  97.1 128.0 %copy-start.13 = (bf16[6,1,448]{2,0,1:T(8,128)(2,1)S(1)}, bf16[6,1,448]{2,0,1:T(8,128)(2,1)}, u32[]{:S(2)}) copy-start(bf16[6,1,448]{2,0,1:T(8,128)(2,1)} %param.19) | copy-start | bytes 16132
  97.1 128.0 %copy-start.16 = (f32[448]{0:T(512)S(1)}, f32[448]{0:T(512)}, u32[]{:S(2)}) copy-start(f32[448]{0:T(512)} %param.23) | copy-start | bytes 5380
  109.8 161.1 %copy-start.14 = (f32[448]{0:T(512)S(1)}, f32[448]{0:T(512)}, u32[]{:S(2)}) copy-start(f32[448]{0:T(512)} %param.24) | copy-start | bytes 5380
  111.8 229.1 %all-reduce.17.cloned.1.call-start = ((), (), s32[]{:S(2)}) async-start(), calls=%async_computation.2 | async-start | bytes 1572864 | tf_op jit(solution)/shard_map/psum | solution.py:143
  205.4 7.6 collective-permute-start
  208.9 4.1 collective-permute-start.1
  272.1 164.2 %copy-start.19 = (u32[256]{0:T(256)S(1)}, u32[256]{0:T(256)}, u32[]{:S(2)}) copy-start(u32[256]{0:T(256)} %constant.109) | copy-start | bytes 3076
  272.1 179.4 %copy-start.17 = (f32[448]{0:T(512)S(1)}, f32[448]{0:T(512)}, u32[]{:S(2)}) copy-start(f32[448]{0:T(512)} %param.25) | copy-start | bytes 5380
  272.1 190.6 %copy-start.18 = (f32[448]{0:T(512)S(1)}, f32[448]{0:T(512)}, u32[]{:S(2)}) copy-start(f32[448]{0:T(512)} %param.26) | copy-start | bytes 5380
  272.1 239.0 %copy-start.4 = (bf16[4,448,112]{2,1,0:T(8,128)(2,1)S(1)}, bf16[4,448,112]{2,1,0:T(8,128)(2,1)}, u32[]{:S(2)}) copy-start(bf16[4,448,112]{2,1,0:T(8,128)(2,1)} %param.34) | copy-start | bytes 1204228
  272.2 305.1 %all-reduce.19.cloned.1.call-start = ((), (), s32[]{:S(2)}) async-start(), calls=%async_computation.3 | async-start | bytes 393216 | tf_op jit(solution)/shard_map/psum | solution.py:159
  342.5 234.8 %copy-start.15 = (f32[4,112]{1,0:T(4,128)S(1)}, f32[4,112]{1,0:T(4,128)}, u32[]{:S(2)}) copy-start(f32[4,112]{1,0:T(4,128)} %param.35) | copy-start | bytes 5380
  410.6 14.9 %collective-permute-start.2 = (f32[8,448]{1,0:T(8,128)S(1)}, f32[8,448]{1,0:T(8,128)S(1)}, u32[]{:S(2)}, u32[]{:S(2)}) collective-permute-start(f32[8,448]{1,0:T(8,128)S(1)} %fusion.1), channel_id=1, source_target_pairs={{0,1},{1,2},{2,3},{3,32},{32,33},{33,34},{34,35},{35,64},{64,65},{... | collective-permute-start | bytes 43016
  412.5 19.8 %collective-permute-start.3 = (f32[8,448]{1,0:T(8,128)S(1)}, f32[8,448]{1,0:T(8,128)S(1)}, u32[]{:S(2)}, u32[]{:S(2)}) collective-permute-start(f32[8,448]{1,0:T(8,128)S(1)} %fusion.1), channel_id=1, source_target_pairs={{0,2},{1,3},{2,32},{3,33},{32,34},{33,35},{34,64},{35,65},{64,66},... | collective-permute-start | bytes 43016
  414.5 5.2 collective-permute-start.9
  415.8 21.8 %collective-permute-start.4 = (f32[8,448]{1,0:T(8,128)S(1)}, f32[8,448]{1,0:T(8,128)S(1)}, u32[]{:S(2)}, u32[]{:S(2)}) collective-permute-start(f32[8,448]{1,0:T(8,128)S(1)} %fusion.1), channel_id=1, source_target_pairs={{0,3},{1,32},{2,33},{3,34},{32,35},{33,64},{34,65},{35,66},{64,67}... | collective-permute-start | bytes 43016
  417.7 19.9 %collective-permute-start.5 = (f32[8,448]{1,0:T(8,128)S(1)}, f32[8,448]{1,0:T(8,128)S(1)}, u32[]{:S(2)}, u32[]{:S(2)}) collective-permute-start(f32[8,448]{1,0:T(8,128)S(1)} %fusion.1), channel_id=1, source_target_pairs={{0,32},{1,33},{2,34},{3,35},{32,64},{33,65},{34,66},{35,67},{64,96... | collective-permute-start | bytes 43016
  419.6 17.9 %collective-permute-start.6 = (f32[8,448]{1,0:T(8,128)S(1)}, f32[8,448]{1,0:T(8,128)S(1)}, u32[]{:S(2)}, u32[]{:S(2)}) collective-permute-start(f32[8,448]{1,0:T(8,128)S(1)} %fusion.1), channel_id=1, source_target_pairs={{0,33},{1,34},{2,35},{3,64},{32,65},{33,66},{34,67},{35,96},{64,97... | collective-permute-start | bytes 43016
  425.5 12.1 %collective-permute-start.7 = (f32[8,448]{1,0:T(8,128)S(1)}, f32[8,448]{1,0:T(8,128)S(1)}, u32[]{:S(2)}, u32[]{:S(2)}) collective-permute-start(f32[8,448]{1,0:T(8,128)S(1)} %fusion.1), channel_id=1, source_target_pairs={{0,34},{1,35},{2,64},{3,65},{32,66},{33,67},{34,96},{35,97},{64,98... | collective-permute-start | bytes 43016
  432.4 5.2 collective-permute-start.8
  437.5 141.7 %copy-start.5 = (s32[5,48,4,8]{1,3,2,0:T(8,128)S(1)}, s32[5,48,4,8]{1,3,2,0:T(8,128)}, u32[]{:S(2)}) copy-start(s32[5,48,4,8]{1,3,2,0:T(8,128)} %param.37) | copy-start | bytes 92164
  512.1 106.0 %all-gather.12.cloned.1.call-start = ((), (), s32[]{:S(2)}) async-start(), calls=%async_computation.5 | async-start | bytes 1769472 | tf_op jit(solution)/shard_map/all_gather | solution.py:166
  513.0 67.6 %copy-start.21 = (s32[1,5]{1,0:T(1,128)S(1)}, s32[1,5]{1,0:T(1,128)}, u32[]{:S(2)}) copy-start(s32[1,5]{1,0:T(1,128)} %param.31) | copy-start | bytes 64
  513.0 166.3 %all-gather.10.cloned.1.call-start = ((), (), s32[]{:S(2)}) async-start(), calls=%async_computation.4 | async-start | bytes 7569408 | tf_op jit(solution)/shard_map/all_gather | solution.py:174
  626.9 60.7 %copy-start.6 = (s32[192,5]{0,1:T(8,128)S(1)}, s32[192,5]{0,1:T(8,128)}, u32[]{:S(2)}) copy-start(s32[192,5]{0,1:T(8,128)} %get-tuple-element.43) | copy-start | bytes 11524
  626.9 60.7 %copy-start.7 = (s32[192,5]{0,1:T(8,128)S(1)}, s32[192,5]{0,1:T(8,128)}, u32[]{:S(2)}) copy-start(s32[192,5]{0,1:T(8,128)} %get-tuple-element.44) | copy-start | bytes 11524
  626.9 60.7 %copy-start.8 = (s32[192,5]{0,1:T(8,128)S(1)}, s32[192,5]{0,1:T(8,128)}, u32[]{:S(2)}) copy-start(s32[192,5]{0,1:T(8,128)} %get-tuple-element.45) | copy-start | bytes 11524
  626.9 60.7 %copy-start.9 = (s32[192,5]{0,1:T(8,128)S(1)}, s32[192,5]{0,1:T(8,128)}, u32[]{:S(2)}) copy-start(s32[192,5]{0,1:T(8,128)} %get-tuple-element.46) | copy-start | bytes 11524
  626.9 60.7 %copy-start.10 = (s32[192,5]{0,1:T(8,128)S(1)}, s32[192,5]{0,1:T(8,128)}, u32[]{:S(2)}) copy-start(s32[192,5]{0,1:T(8,128)} %get-tuple-element.47) | copy-start | bytes 11524
  626.9 60.7 %copy-start.11 = (s32[192,5]{0,1:T(8,128)S(1)}, s32[192,5]{0,1:T(8,128)}, u32[]{:S(2)}) copy-start(s32[192,5]{0,1:T(8,128)} %get-tuple-element.48) | copy-start | bytes 11524
  626.9 60.7 %copy-start.12 = (s32[192,5]{0,1:T(8,128)S(1)}, s32[192,5]{0,1:T(8,128)}, u32[]{:S(2)}) copy-start(s32[192,5]{0,1:T(8,128)} %get-tuple-element.49) | copy-start | bytes 11524
Sparse Core Ops, SparseCore 0:
  26.3 68.1 all-reduce.12
  111.9 73.9 all-reduce.14
  272.3 68.5 all-reduce.16
  512.2 65.0 all-reduce.18
  578.9 39.1 all-gather.11
  620.5 58.7 all-gather.9
